TPU v7x, 32 devices: a whole 2x2x4 slice. The times are simulated.
32 devices in a mesh: row: 4 (over y, x), col: 8 (over z, core).
Axes of the slice: x: 2, y: 2, z: 4, core: 2. Of those that a mesh axis runs over, the one named last changes fastest.
Arguments:
- trailing_slab: bfloat16 [24576, 8192], P('row', 'col'), may hold values from -6 to 6
- panel_cols: bfloat16 [24576, 512], P('row', 'col'), may hold values from -0.25 to 0.25
- head_slab: bfloat16 [512, 8192], P('row', 'col'), may hold values from -6 to 6
- coupling: bfloat16 [2, 256, 256], replicated, may hold values from -0.25 to 0.25
- lower_inverses: bfloat16 [2, 256, 256], replicated, may hold values from -1.5 to 1.5, as said below
- upper_inverses: bfloat16 [2, 256, 256], replicated, may hold values from -1.5 to 1.5, as said below
Outputs:
- trailing: bfloat16 [24576, 8192], P('row', 'col')
Inputs may be any that keep to these rules, and one draw needn't show every extreme that they name: `lower_inverses`: each of the two [256, 256] blocks is lower triangular with unit diagonal. `upper_inverses`: each of the two [256, 256] blocks is upper triangular with diagonal between 0.5 and 1.5.
All inputs are finite; a program needn't handle non-finite values.
Results may differ from a plain program's by a relative error of at most 0.0067.
Values may be sent and summed in bfloat16 or wider, within the bound.
No kernel may reach another device: no remote copies, remote signals or barrier semaphores. Data moves between devices by JAX's collectives and lax.ppermute only.
A program may use at most 128 MiB of HBM per device.

v0:
```python
import jax
import jax.numpy as jnp
from jax import lax
from jax.sharding import PartitionSpec as P


def product(left, right):
    return jnp.dot(left, right, preferred_element_type=jnp.float32)


def factor_panel(panel_block, upper_mid, upper_inverses):
    width = upper_mid.shape[0]
    lower_first = product(panel_block[:, :width], upper_inverses[0]).astype(jnp.bfloat16)
    panel_second = (
        panel_block[:, width:].astype(jnp.float32) - product(lower_first, upper_mid)
    ).astype(jnp.bfloat16)
    lower_second = product(panel_second, upper_inverses[1]).astype(jnp.bfloat16)
    return jnp.concatenate([lower_first, lower_second], axis=1)


def apply_update(slab_part, lower_block, upper_both):
    result = slab_part.astype(jnp.float32) - product(lower_block, upper_both)
    return result.astype(jnp.bfloat16)


def on_device(trailing_slab, panel_cols, head_slab, coupling, lower_inverses, upper_inverses):
    width = coupling.shape[1]
    head_full = lax.all_gather(head_slab, "row", axis=0, tiled=True)
    upper_mid = product(lower_inverses[0], coupling[0]).astype(jnp.bfloat16)
    upper_first = product(lower_inverses[0], head_full[:width]).astype(jnp.bfloat16)
    lower_head = product(coupling[1], upper_inverses[0]).astype(jnp.bfloat16)
    head_second = (head_full[width:].astype(jnp.float32) - product(lower_head, upper_first)).astype(
        jnp.bfloat16
    )
    upper_second = product(lower_inverses[1], head_second).astype(jnp.bfloat16)
    upper_both = jnp.concatenate([upper_first, upper_second], axis=0)
    panel_full = lax.all_gather(panel_cols, "col", axis=1, tiled=True)
    lower_block = factor_panel(panel_full, upper_mid, upper_inverses)
    return apply_update(trailing_slab, lower_block, upper_both)


def solution(mesh):
    in_specs = (P("row", "col"), P("row", "col"), P("row", "col"), P(), P(), P())
    out_specs = P("row", "col")
    return jax.shard_map(
        on_device, mesh=mesh, in_specs=in_specs, out_specs=out_specs, check_vma=False
    )
```

profile of v0, /device:TPU:0, one launch (start us, length us, event | category | flops | bytes accessed | tf_op | source)
XLA Modules:
  0.0 133.2 jit_solution(17150895435019928692)
XLA Ops:
  6.5 0.0 all-gather.5.cloned.1.call-start
  6.5 0.7 all-gather.5.cloned.1.call-update
  7.3 0.0 all-gather.3.cloned.1.call-start
  7.3 0.7 all-gather.3.cloned.1.call-update
  8.0 1.2 convolution_convert_fusion.4
  9.2 1.2 convolution_convert_fusion.5
  10.3 0.0 copy-start.1
  10.3 28.1 %all-gather.5.cloned.1.call-done = bf16[512,1024]{1,0:T(8,128)(2,1)} async-done(((bf16[128,1024]{1,0:T(8,128)(2,1)}), bf16[512,1024]{1,0:T(8,128)(2,1)}) %all-gather.5.cloned.1.call-update) | async-done | bytes 1048592 | tf_op jit(solution)/shard_map/all_gather | solution.py:28
  38.4 1.4 %convolution_convert_fusion.3 = bf16[256,1024]{1,0:T(8,128)(2,1)S(1)} fusion(bf16[512,1024]{1,0:T(8,128)(2,1)} %all-gather.5.cloned.1.call-done, bf16[2,256,256]{2,1,0:T(8,128)(2,1)} %param.10), kind=kOutput, calls=%fused_computation.11 | convolution fusion | flops 134479872 | bytes 1179648 | tf_op jit(solution)/shard_map/dot_general | solution.py:8
  39.9 0.0 copy-start
  39.9 2.6 %fusion.6 = bf16[256,1024]{1,0:T(8,128)(2,1)} fusion(bf16[256,256]{1,0:T(8,128)(2,1)S(1)} %convolution_convert_fusion.4, bf16[256,1024]{1,0:T(8,128)(2,1)S(1)} %convolution_convert_fusion.3, bf16[512,1024]{1,0:T(8,128)(2,1)} %all-gather.5.cloned.1.call-done, bf16[2,256,256]{2,1,0:T(8,128)(2,1)} %param.10), kind=kOutput, calls=%fused_computation.13 | convolution fusion | flops 269484032 | bytes 1835008 | tf_op jit(solution)/shard_map/dot_general | solution.py:8
  42.5 0.0 copy-done
  42.5 62.3 %all-gather.3.cloned.1.call-done = bf16[6144,512]{0,1:T(8,128)(2,1)} async-done(((bf16[6144,64]{0,1:T(8,128)(2,1)}), bf16[6144,512]{0,1:T(8,128)(2,1)}) %all-gather.3.cloned.1.call-update) | async-done | bytes 6291472 | tf_op jit(solution)/shard_map/all_gather | solution.py:37
  104.8 2.9 %convolution_convert_fusion.1 = bf16[6144,256]{0,1:T(8,128)(2,1)S(1)} fusion(bf16[6144,512]{0,1:T(8,128)(2,1)} %all-gather.3.cloned.1.call-done, bf16[2,256,256]{2,1,0:T(8,128)(2,1)} %param.11), kind=kOutput, calls=%fused_computation.4 | convolution fusion | flops 806879232 | bytes 6422528 | tf_op jit(solution)/shard_map/dot_general | solution.py:8
  107.7 0.0 copy-done.1
  107.7 5.5 %convolution_convert_fusion = bf16[6144,256]{0,1:T(8,128)(2,1)} fusion(bf16[6144,256]{0,1:T(8,128)(2,1)S(1)} %convolution_convert_fusion.1, bf16[256,256]{1,0:T(8,128)(2,1)S(1)} %convolution_convert_fusion.5, bf16[6144,512]{0,1:T(8,128)(2,1)} %all-gather.3.cloned.1.call-done, bf16[2,256,256]{2,1,0:T(8,128)(2,1)S(1)} %copy-done.1), kind=kOutput, calls=%fused_computation.3 | convolution fusion | flops 1616904192 | bytes 9699328 | tf_op jit(solution)/shard_map/dot_general | solution.py:8
  113.2 13.2 %subtract_convert_fusion = bf16[6144,1024]{1,0:T(8,128)(2,1)} fusion(bf16[6144,1024]{1,0:T(8,128)(2,1)} %param.6, bf16[6144,256]{0,1:T(8,128)(2,1)} %convolution_convert_fusion, bf16[6144,256]{0,1:T(8,128)(2,1)S(1)} %convolution_convert_fusion.1, bf16[256,1024]{1,0:T(8,128)(2,1)} %fusion.6, bf16[256,1024]{1,0:T(8,128)(2,1)} %copy-done), kind=kOutput, calls=%fused_computation | convolution fusion | flops 6476005376 | bytes 32505856 | tf_op jit(solution)/shard_map/dot_general | solution.py:8
Async XLA Ops:
  6.5 31.9 %all-gather.5.cloned.1.call-start = ((), (), s32[]{:S(2)}) async-start(), calls=%async_computation.1 | async-start | bytes 1310720 | tf_op jit(solution)/shard_map/all_gather | solution.py:28
  7.3 97.5 %all-gather.3.cloned.1.call-start = ((), (), s32[]{:S(2)}) async-start(), calls=%async_computation | async-start | bytes 7077888 | tf_op jit(solution)/shard_map/all_gather | solution.py:37
  10.3 97.4 %copy-start.1 = (bf16[2,256,256]{2,1,0:T(8,128)(2,1)S(1)}, bf16[2,256,256]{2,1,0:T(8,128)(2,1)}, u32[]{:S(2)}) copy-start(bf16[2,256,256]{2,1,0:T(8,128)(2,1)} %param.11) | copy-start | bytes 786436
  39.9 2.6 %copy-start = (bf16[256,1024]{1,0:T(8,128)(2,1)}, bf16[256,1024]{1,0:T(8,128)(2,1)S(1)}, u32[]{:S(2)}) copy-start(bf16[256,1024]{1,0:T(8,128)(2,1)S(1)} %convolution_convert_fusion.3) | copy-start | bytes 1572868
Sparse Core Ops, SparseCore 0:
  9.2 29.2 all-gather.4
  40.1 64.6 all-gather.2
where the time goes:
time: 133 us
  waiting for transfers between devices  91.8 us (69%)
  matrix products  27.9 us (21%)
  between operations  13.5 us (10%)
    all_gather x1, waiting for transfers between devices, on_device(): panel_full = lax.all_gather(panel_cols, 'col', axis=1, tiled=True)  62.3 us
    all_gather x1, waiting for transfers between devices, on_device(): head_full = lax.all_gather(head_slab, 'row', axis=0, tiled=True)  28.1 us
    dot_general x7, matrix products, product(): return jnp.dot(left, right, preferred_element_type=jnp.float32)  27.9 us
  transfers between devices with their start and end apart: 2, of which 2 were waited for; matrix products, arithmetic and copies ran while one was open for 5% of the time, Pallas kernels for 0%

commit v1 on v0

--- a/solution.py
+++ b/solution.py
@@ -2,6 +2,38 @@
 import jax.numpy as jnp
 from jax import lax
 from jax.sharding import PartitionSpec as P
+
+
+def _pair_table(row_data, array_axis):
+    row_data = jnp.moveaxis(row_data, 0, array_axis)
+    current_arr = row_data.shape
+    seen_now = row_data.reshape(
+        *current_arr[:array_axis],
+        current_arr[array_axis] * current_arr[array_axis + 1],
+        *current_arr[array_axis + 2 :]
+    )
+    return seen_now
+
+
+def time_the_panels(vec, comm_axis):
+    lower = lax.psum(1, axis_name=comm_axis)
+    then = lax.axis_index(comm_axis)
+    z2, a_now = (lower, then)
+    s_next, answer = (vec[None], 1)
+    while answer < z2:
+        f_now = lax.ppermute(s_next, axis_name=comm_axis, perm=[(d, d ^ answer) for d in range(z2)])
+        p_next = a_now & answer == 0
+        part_next = jnp.where(p_next, s_next, f_now)
+        u_next = jnp.where(p_next, f_now, s_next)
+        s_next = jnp.concatenate([part_next, u_next])
+        answer *= 2
+    return s_next
+
+
+def meet_the_node(u, q_in, dim_at):
+    inter = time_the_panels(u, q_in)
+    later = _pair_table(inter, dim_at)
+    return later
 
 
 def product(left, right):
@@ -25,7 +57,7 @@
 
 def on_device(trailing_slab, panel_cols, head_slab, coupling, lower_inverses, upper_inverses):
     width = coupling.shape[1]
-    head_full = lax.all_gather(head_slab, "row", axis=0, tiled=True)
+    head_full = meet_the_node(head_slab, "row", 0)
     upper_mid = product(lower_inverses[0], coupling[0]).astype(jnp.bfloat16)
     upper_first = product(lower_inverses[0], head_full[:width]).astype(jnp.bfloat16)
     lower_head = product(coupling[1], upper_inverses[0]).astype(jnp.bfloat16)

time: 133 us -> 105 us (0.79)
  waiting for transfers between devices: 91.8 us -> 59.9 us
  starting transfers between devices: 0.04 us -> 4.87 us
  matrix products: 27.9 us -> 25.5 us
    all_gather x1 -> x0, waiting for transfers between devices: 28.1 us -> none  [on_device(): head_full = lax.all_gather(head_slab, 'row', axis=0, tiled=True)]
    all_gather x1, waiting for transfers between devices: 62.3 us -> 42.5 us  [on_device(): panel_full = lax.all_gather(panel_cols, 'col', axis=1, tiled=True)]
    ppermute x0 -> x2, waiting for transfers between devices: none -> 16.7 us  [time_the_panels(): lax.ppermute(s_next, axis_name=comm_axis, perm=[(d, d ^ answer) for d in...]
    ppermute x0 -> x2, starting transfers between devices: none -> 4.87 us  [time_the_panels(): lax.ppermute(s_next, axis_name=comm_axis, perm=[(d, d ^ answer) for d in...]
    dot_general x7, matrix products: 27.9 us -> 25.5 us  [product(): return jnp.dot(left, right, preferred_element_type=jnp.float32)]
  transfers between devices with their start and end apart: 2 -> 3, of which waited for: 2 -> 3; matrix products, arithmetic and copies ran while one was open for 5% -> 5% of each run, Pallas kernels for 0% -> 0%
where the time goes in v1:
time: 105 us
  waiting for transfers between devices  59.9 us (57%)
  matrix products  25.5 us (24%)
  between operations  13.5 us (13%)
  starting transfers between devices  4.87 us (5%)
  other arithmetic  1.11 us (1%)
    all_gather x1, waiting for transfers between devices, on_device(): panel_full = lax.all_gather(panel_cols, 'col', axis=1, tiled=True)  42.5 us
    dot_general x7, matrix products, product(): return jnp.dot(left, right, preferred_element_type=jnp.float32)  25.5 us
    ppermute x2, waiting for transfers between devices, time_the_panels(): lax.ppermute(s_next, axis_name=comm_axis, perm=[(d, d ^ answer) for d in...  16.7 us
    ppermute x2, starting transfers between devices, time_the_panels(): lax.ppermute(s_next, axis_name=comm_axis, perm=[(d, d ^ answer) for d in...  4.87 us
  transfers between devices with their start and end apart: 3, of which 3 were waited for; matrix products, arithmetic and copies ran while one was open for 5% of the time, Pallas kernels for 0%

profile of v1, /device:TPU:0, one launch (start us, length us, event | category | flops | bytes accessed | tf_op | source)
XLA Modules:
  0.0 104.9 jit_solution(8720201910342270022)
XLA Ops:
  6.5 0.0 copy-start.1
  6.5 0.0 copy-start.3
  6.5 0.0 all-gather.2.cloned.1.call-start
  6.5 0.7 all-gather.2.cloned.1.call-update
  7.3 3.0 %collective-permute-start = (bf16[1,128,1024]{2,1,0:T(8,128)(2,1)}, bf16[1,128,1024]{2,1,0:T(8,128)(2,1)S(1)}, u32[]{:S(2)}, u32[]{:S(2)}) collective-permute-start(bf16[1,128,1024]{2,1,0:T(8,128)(2,1)} %bitcast.40), channel_id=1, source_target_pairs={{0,8},{8,0},{16,24},{24,16},{1,9},{9,1},{17,25},{25,17},{2,10},{10... | collective-permute-start | bytes 786440 | tf_op jit(solution)/shard_map/ppermute | solution.py:24
  10.3 6.5 %collective-permute-done = bf16[1,128,1024]{2,1,0:T(8,128)(2,1)S(1)} collective-permute-done((bf16[1,128,1024]{2,1,0:T(8,128)(2,1)}, bf16[1,128,1024]{2,1,0:T(8,128)(2,1)S(1)}, u32[]{:S(2)}, u32[]{:S(2)}) %collective-permute-start) | collective-permute-done | bytes 262176 | tf_op jit(solution)/shard_map/ppermute | solution.py:24
  16.8 1.0 broadcast_select_fusion.3
  17.8 0.1 pad_maximum_fusion
  17.9 1.8 %collective-permute-start.1 = (bf16[2,128,1024]{2,1,0:T(8,128)(2,1)S(1)}, bf16[2,128,1024]{2,1,0:T(8,128)(2,1)S(1)}, u32[]{:S(2)}, u32[]{:S(2)}) collective-permute-start(bf16[2,128,1024]{2,1,0:T(8,128)(2,1)S(1)} %pad_maximum_fusion), channel_id=1, source_target_pairs={{0,16},{8,24},{16,0},{24,8},{1,17},{9,25},{17,1},{25,9},{2,18},{10... | collective-permute-start | bytes 1572872 | tf_op jit(solution)/shard_map/ppermute | solution.py:24
  19.7 1.2 %convolution_convert_fusion.5 = bf16[256,256]{1,0:T(8,128)(2,1)S(1)} fusion(bf16[2,256,256]{2,1,0:T(8,128)(2,1)} %param.9, bf16[2,256,256]{2,1,0:T(8,128)(2,1)} %param.10), kind=kOutput, calls=%fused_computation.13 | convolution fusion | flops 33619968 | bytes 393216 | tf_op jit(solution)/shard_map/dot_general | solution.py:40
  20.9 10.2 %collective-permute-done.1 = bf16[2,128,1024]{2,1,0:T(8,128)(2,1)S(1)} collective-permute-done((bf16[2,128,1024]{2,1,0:T(8,128)(2,1)S(1)}, bf16[2,128,1024]{2,1,0:T(8,128)(2,1)S(1)}, u32[]{:S(2)}, u32[]{:S(2)}) %collective-permute-start.1) | collective-permute-done | bytes 524320 | tf_op jit(solution)/shard_map/ppermute | solution.py:24
  31.0 0.1 broadcast_select_fusion
  31.1 1.2 %convolution_convert_fusion.3 = bf16[1024,256]{0,1:T(8,128)(2,1)S(1)} fusion(bf16[256,1024]{1,0:T(8,128)(2,1)S(1)} %bitcast.39, bf16[2,256,256]{2,1,0:T(8,128)(2,1)} %param.10), kind=kOutput, calls=%fused_computation.10 | convolution fusion | flops 134479872 | bytes 1179648 | tf_op jit(solution)/shard_map/dot_general | solution.py:40
  32.3 0.0 copy-done.3
  32.3 0.0 copy-done.2
  32.3 0.0 copy-start
  32.3 0.4 fusion.6
  32.8 0.0 copy-done.1
  32.8 1.1 %fusion.5 = bf16[256,1024]{1,0:T(8,128)(2,1)} fusion(f32[256,1024]{1,0:T(8,128)S(1)} %fusion.6, bf16[256,1024]{1,0:T(8,128)(2,1)S(1)} %bitcast.37, bf16[2,256,256]{2,1,0:T(8,128)(2,1)S(1)} %copy-done.1), kind=kOutput, calls=%fused_computation.11 | convolution fusion | flops 135266304 | bytes 2228224 | tf_op jit(solution)/shard_map/dot_general | solution.py:40
  33.9 0.0 copy-done
  33.9 42.5 %all-gather.2.cloned.1.call-done = bf16[6144,512]{0,1:T(8,128)(2,1)} async-done(((bf16[6144,64]{0,1:T(8,128)(2,1)}), bf16[6144,512]{0,1:T(8,128)(2,1)}) %all-gather.2.cloned.1.call-update) | async-done | bytes 6291472 | tf_op jit(solution)/shard_map/all_gather | solution.py:69
  76.4 2.9 %convolution_convert_fusion.1 = bf16[6144,256]{0,1:T(8,128)(2,1)S(1)} fusion(bf16[6144,512]{0,1:T(8,128)(2,1)} %all-gather.2.cloned.1.call-done, bf16[2,256,256]{2,1,0:T(8,128)(2,1)} %param.11), kind=kOutput, calls=%fused_computation.4 | convolution fusion | flops 806879232 | bytes 6422528 | tf_op jit(solution)/shard_map/dot_general | solution.py:40
  79.3 5.5 %convolution_convert_fusion = bf16[6144,256]{0,1:T(8,128)(2,1)} fusion(bf16[6144,256]{0,1:T(8,128)(2,1)S(1)} %convolution_convert_fusion.1, bf16[256,256]{1,0:T(8,128)(2,1)S(1)} %convolution_convert_fusion.5, bf16[6144,512]{0,1:T(8,128)(2,1)} %all-gather.2.cloned.1.call-done, bf16[2,256,256]{2,1,0:T(8,128)(2,1)} %param.11), kind=kOutput, calls=%fused_computation.3 | convolution fusion | flops 1616904192 | bytes 9699328 | tf_op jit(solution)/shard_map/dot_general | solution.py:40
  84.8 13.2 %subtract_convert_fusion = bf16[6144,1024]{1,0:T(8,128)(2,1)} fusion(bf16[6144,1024]{1,0:T(8,128)(2,1)} %param.6, bf16[6144,256]{0,1:T(8,128)(2,1)} %convolution_convert_fusion, bf16[6144,256]{0,1:T(8,128)(2,1)S(1)} %convolution_convert_fusion.1, bf16[256,1024]{1,0:T(8,128)(2,1)} %fusion.5, bf16[256,1024]{1,0:T(8,128)(2,1)} %bitcast.38), kind=kOutput, calls=%fused_computation | convolution fusion | flops 6476005376 | bytes 32505856 | tf_op jit(solution)/shard_map/dot_general | solution.py:40
  (1 shorter events, 0.0 us)
Async XLA Ops:
  6.5 26.2 %copy-start.1 = (bf16[2,256,256]{2,1,0:T(8,128)(2,1)S(1)}, bf16[2,256,256]{2,1,0:T(8,128)(2,1)}, u32[]{:S(2)}) copy-start(bf16[2,256,256]{2,1,0:T(8,128)(2,1)} %param.10) | copy-start | bytes 786436
  6.5 25.8 %copy-start.3 = (bf16[2,256,256]{2,1,0:T(8,128)(2,1)S(1)}, bf16[2,256,256]{2,1,0:T(8,128)(2,1)}, u32[]{:S(2)}) copy-start(bf16[2,256,256]{2,1,0:T(8,128)(2,1)} %param.9) | copy-start | bytes 786436
  6.5 25.8 %copy-start.2 = (bf16[2,256,256]{2,1,0:T(8,128)(2,1)S(1)}, bf16[2,256,256]{2,1,0:T(8,128)(2,1)}, u32[]{:S(2)}) copy-start(bf16[2,256,256]{2,1,0:T(8,128)(2,1)} %param.11) | copy-start | bytes 786436
  6.5 69.9 %all-gather.2.cloned.1.call-start = ((), (), s32[]{:S(2)}) async-start(), calls=%async_computation | async-start | bytes 7077888 | tf_op jit(solution)/shard_map/all_gather | solution.py:69
  7.3 9.5 %collective-permute-start = (bf16[1,128,1024]{2,1,0:T(8,128)(2,1)}, bf16[1,128,1024]{2,1,0:T(8,128)(2,1)S(1)}, u32[]{:S(2)}, u32[]{:S(2)}) collective-permute-start(bf16[1,128,1024]{2,1,0:T(8,128)(2,1)} %bitcast.40), channel_id=1, source_target_pairs={{0,8},{8,0},{16,24},{24,16},{1,9},{9,1},{17,25},{25,17},{2,10},{10... | collective-permute-start | bytes 786440 | tf_op jit(solution)/shard_map/ppermute | solution.py:24
  17.9 13.2 %collective-permute-start.1 = (bf16[2,128,1024]{2,1,0:T(8,128)(2,1)S(1)}, bf16[2,128,1024]{2,1,0:T(8,128)(2,1)S(1)}, u32[]{:S(2)}, u32[]{:S(2)}) collective-permute-start(bf16[2,128,1024]{2,1,0:T(8,128)(2,1)S(1)} %pad_maximum_fusion), channel_id=1, source_target_pairs={{0,16},{8,24},{16,0},{24,8},{1,17},{9,25},{17,1},{25,9},{2,18},{10... | collective-permute-start | bytes 1572872 | tf_op jit(solution)/shard_map/ppermute | solution.py:24
  32.3 1.6 %copy-start = (bf16[1024,256]{0,1:T(8,128)(2,1)}, bf16[1024,256]{0,1:T(8,128)(2,1)S(1)}, u32[]{:S(2)}) copy-start(bf16[1024,256]{0,1:T(8,128)(2,1)S(1)} %convolution_convert_fusion.3) | copy-start | bytes 1572868
Sparse Core Ops, SparseCore 0:
  9.0 67.4 all-gather.1
